TPU v7x, 256 devices: a whole 4x4x8 slice. The times are simulated.
256 devices in a mesh: ctx: 8 (over z), exp: 32 (over y, x, core).
Axes of the slice: x: 4, y: 4, z: 8, core: 2. Of those that a mesh axis runs over, the one named last changes fastest.
Arguments:
- query_rows: bfloat16 [6144, 4096], P('ctx', 'exp'), may hold values from -6 to 6
- key_rows: bfloat16 [6144, 4096], P('ctx', 'exp'), may hold values from -6 to 6
- value_rows: bfloat16 [6144, 4096], P('ctx', 'exp'), may hold values from -6 to 6
- log_decay: float32 [32, 6144], P('exp', 'ctx'), may hold values from -1 to 0
- residual: bfloat16 [6144, 3072], P(('ctx', 'exp')), may hold values from -20 to 20
- norm_gain: float32 [3072], replicated, may hold values from 0.1 to 1.9
- out_grad: bfloat16 [6144, 3072], P(('ctx', 'exp')), may hold values from -6 to 6
- experts_of: int32 [6144, 2], P(('ctx', 'exp')), may hold values from 0 to 31, all different within a row; in each aligned block of 24 rows (0 to 23, 24 to 47, ...) at most 2 rows name the same one
- route_weight: float32 [6144, 2], P(('ctx', 'exp')), may hold values from 0.1 to 0.9
- output_weight: bfloat16 [4096, 3072], P('exp'), may hold values from -0.09375 to 0.09375
- expert_gate: bfloat16 [32, 3072, 4608], P('exp', None, 'ctx'), may hold values from -0.109375 to 0.109375
- expert_up: bfloat16 [32, 3072, 4608], P('exp', None, 'ctx'), may hold values from -0.109375 to 0.109375
- expert_down: bfloat16 [32, 4608, 3072], P('exp', 'ctx'), may hold values from -0.09375 to 0.09375
Outputs:
- query_grad: bfloat16 [6144, 4096], P('ctx', 'exp')
- key_grad: bfloat16 [6144, 4096], P('ctx', 'exp')
- value_grad: bfloat16 [6144, 4096], P('ctx', 'exp')
Inputs may be any that keep to these rules, and one draw needn't show every extreme that they name: `experts_of`: in each aligned block of 24 tokens (the tokens of one device) no expert is named by more than 2 tokens, a bound that some block reaches; a token's two experts differ.
All inputs are finite; a program needn't handle non-finite values.
Results may differ from a plain program's by a relative error of at most 0.017.
Values may be sent and summed in bfloat16 or wider, within the bound.
No kernel may reach another device: no remote copies, remote signals or barrier semaphores. Data moves between devices by JAX's collectives and lax.ppermute only.
A program may use at most 128 MiB of HBM per device.

v0:
```python
import math
import jax
import jax.numpy as jnp
from jax import lax
from jax.sharding import PartitionSpec as P


def prefix(part, axis, combine, identity, reverse):
    count = lax.axis_size(axis)
    place = lax.axis_index(axis)
    ahead = count - 1 - place if reverse else place
    gathered = jax.tree.map(lambda a: lax.all_gather(a, axis), part)
    state = jax.tree.map(lambda a, e: jnp.zeros_like(a) + jnp.asarray(e, a.dtype), part, identity)

    def one(turn, state):
        source = count - 1 - turn if reverse else turn
        return combine(
            state, jax.tree.map(lambda a: lax.dynamic_index_in_dim(a, source, 0, False), gathered)
        )

    return lax.fori_loop(0, ahead, one, state)


def normalize(residual, norm_gain):
    residual_f = residual.astype(jnp.float32)
    factor = lax.rsqrt(jnp.mean(residual_f * residual_f, axis=-1, keepdims=True) + 1e-05)
    return (residual_f, factor, (residual_f * factor * norm_gain).astype(jnp.bfloat16))


def slot_table(experts_of, count, capacity):
    flat_ids = experts_of.reshape(-1)
    matches = (flat_ids[:, None] == jnp.arange(count, dtype=jnp.int32)[None, :]).astype(jnp.int32)
    before = jnp.cumsum(matches, axis=0, dtype=jnp.int32) - matches
    target = flat_ids * capacity + jnp.sum(before * matches, axis=1, dtype=jnp.int32)
    slots = jnp.arange(count * capacity, dtype=jnp.int32)
    return (slots[:, None] == target[None, :]).astype(jnp.bfloat16)


def expert_rows(row_block, gate_mat, up_mat, down_mat):
    features = gate_mat.shape[0]
    row_input = row_block[:, :features]
    row_grad = row_block[:, features:]
    gate_pre = jnp.dot(row_input, gate_mat, preferred_element_type=jnp.float32)
    up_pre = jnp.dot(row_input, up_mat, preferred_element_type=jnp.float32)
    hidden_grad = lax.dot_general(
        row_grad, down_mat, (((1,), (1,)), ((), ())), preferred_element_type=jnp.float32
    )
    gate_sig = jax.nn.sigmoid(gate_pre)
    gate_grad = (hidden_grad * up_pre * gate_sig * (1.0 + gate_pre * (1.0 - gate_sig))).astype(
        jnp.bfloat16
    )
    up_grad = (hidden_grad * gate_pre * gate_sig).astype(jnp.bfloat16)
    first = lax.dot_general(
        gate_grad, gate_mat, (((1,), (1,)), ((), ())), preferred_element_type=jnp.float32
    )
    second = lax.dot_general(
        up_grad, up_mat, (((1,), (1,)), ((), ())), preferred_element_type=jnp.float32
    )
    return first + second


def block_terms(query_part, key_part, value_part, grad_part, log_steps, score_scale):
    levels = jnp.cumsum(log_steps)
    block_total = levels[-1]
    from_start = jnp.exp(levels)
    to_end = jnp.exp(block_total - levels)
    key_state = lax.dot_general(
        key_part.astype(jnp.float32) * to_end[:, None],
        value_part.astype(jnp.float32),
        (((0,), (0,)), ((), ())),
        precision=lax.Precision.HIGHEST,
    )
    adjoint = score_scale * lax.dot_general(
        query_part.astype(jnp.float32) * from_start[:, None],
        grad_part.astype(jnp.float32),
        (((0,), (0,)), ((), ())),
        precision=lax.Precision.HIGHEST,
    )
    return (levels, jnp.exp(block_total), key_state, adjoint)


def block_grads(
    query_part, key_part, value_part, grad_part, levels, state_in, adjoint_out, score_scale
):
    block_total = levels[-1]
    from_start = jnp.exp(levels)
    to_end = jnp.exp(block_total - levels)
    token_position = jnp.arange(levels.shape[0], dtype=jnp.int32)
    causal = token_position[:, None] >= token_position[None, :]
    fading = jnp.exp(jnp.where(causal, levels[:, None] - levels[None, :], -jnp.inf))
    scores = lax.dot_general(
        query_part, key_part, (((1,), (1,)), ((), ())), preferred_element_type=jnp.float32
    )
    attn_probs = (score_scale * scores * fading).astype(jnp.bfloat16)
    grad_scores = lax.dot_general(
        grad_part, value_part, (((1,), (1,)), ((), ())), preferred_element_type=jnp.float32
    )
    pull_weights = (score_scale * grad_scores * fading).astype(jnp.bfloat16)
    grad_f = grad_part.astype(jnp.float32)
    query_out = jnp.dot(pull_weights, key_part, preferred_element_type=jnp.float32)
    query_out = query_out + score_scale * from_start[:, None] * lax.dot_general(
        grad_f, state_in, (((1,), (1,)), ((), ())), precision=lax.Precision.HIGHEST
    )
    key_out = lax.dot_general(
        pull_weights, query_part, (((0,), (0,)), ((), ())), preferred_element_type=jnp.float32
    )
    key_out = key_out + to_end[:, None] * lax.dot_general(
        value_part.astype(jnp.float32),
        adjoint_out,
        (((1,), (1,)), ((), ())),
        precision=lax.Precision.HIGHEST,
    )
    value_out = lax.dot_general(
        attn_probs, grad_part, (((0,), (0,)), ((), ())), preferred_element_type=jnp.float32
    )
    value_out = value_out + to_end[:, None] * jnp.dot(
        key_part.astype(jnp.float32), adjoint_out, precision=lax.Precision.HIGHEST
    )
    return (
        query_out.astype(jnp.bfloat16),
        key_out.astype(jnp.bfloat16),
        value_out.astype(jnp.bfloat16),
    )


def chain_link(earlier, following):
    return (earlier[0] * following[0], following[0] * earlier[1] + following[1])


def body(
    query_rows,
    key_rows,
    value_rows,
    log_decay,
    residual,
    norm_gain,
    out_grad,
    experts_of,
    route_weight,
    output_weight,
    expert_gate,
    expert_up,
    expert_down,
):
    ctx_count = lax.axis_size("ctx")
    exp_count = lax.axis_size("exp")
    token_count = residual.shape[0]
    features = residual.shape[1]
    capacity = max(2, 3 * token_count // exp_count)
    residual_f, factor, expert_input = normalize(residual, norm_gain)
    slot_onehot = slot_table(experts_of, exp_count, capacity)
    routed = (route_weight[:, :, None] * out_grad.astype(jnp.float32)[:, None, :]).astype(
        jnp.bfloat16
    )
    inputs = jnp.broadcast_to(expert_input[:, None, :], routed.shape)
    packed = jnp.concatenate([inputs, routed], axis=-1).reshape(2 * token_count, 2 * features)
    outgoing = jnp.dot(slot_onehot, packed, preferred_element_type=jnp.float32).astype(jnp.bfloat16)
    outgoing = outgoing.reshape(exp_count, capacity, 2 * features)
    gate_mat = expert_gate[0]
    up_mat = expert_up[0]
    down_mat = expert_down[0]
    arrived = lax.all_to_all(outgoing, "exp", split_axis=0, concat_axis=0, tiled=True).reshape(
        exp_count * capacity, 2 * features
    )
    partials = expert_rows(
        lax.all_gather(arrived, "ctx", axis=0, tiled=True), gate_mat, up_mat, down_mat
    )
    partials = partials.reshape(ctx_count, exp_count, capacity, features)
    summed = lax.psum_scatter(
        partials.astype(jnp.bfloat16), "ctx", scatter_dimension=0, tiled=True
    ).astype(jnp.float32)
    returned = lax.all_to_all(
        summed[0].astype(jnp.bfloat16), "exp", split_axis=0, concat_axis=0, tiled=True
    )
    per_row = lax.dot_general(
        slot_onehot,
        returned.reshape(exp_count * capacity, features),
        (((0,), (0,)), ((), ())),
        preferred_element_type=jnp.float32,
    )
    moe_grad = jnp.sum(per_row.reshape(token_count, 2, features), axis=1)
    scaled = norm_gain * moe_grad
    unit_rows = residual_f * factor
    total_grad = out_grad.astype(jnp.float32) + factor * (
        scaled - unit_rows * jnp.mean(unit_rows * scaled, axis=-1, keepdims=True)
    )
    resid_grad = total_grad.astype(jnp.bfloat16)
    attn_grad = lax.dot_general(
        lax.all_gather(resid_grad, "exp", axis=0, tiled=True),
        output_weight,
        (((1,), (1,)), ((), ())),
        preferred_element_type=jnp.float32,
    ).astype(jnp.bfloat16)
    block_len = query_rows.shape[0]
    head_size = query_rows.shape[1]
    score_scale = 1.0 / math.sqrt(head_size * block_len * ctx_count)
    levels, block_gain, key_state, adjoint = block_terms(
        query_rows, key_rows, value_rows, attn_grad, log_decay[0], score_scale
    )
    zero_state = jnp.zeros((head_size, head_size), jnp.float32)
    identity = (jnp.ones((), jnp.float32), zero_state)
    state_pair = prefix((block_gain, key_state), "ctx", chain_link, identity, False)
    adjoint_pair = prefix((block_gain, adjoint), "ctx", chain_link, identity, True)
    state_in = state_pair[1]
    adjoint_out = adjoint_pair[1]
    return block_grads(
        query_rows, key_rows, value_rows, attn_grad, levels, state_in, adjoint_out, score_scale
    )


def solution(mesh):
    placed = (
        P("ctx", "exp"),
        P("ctx", "exp"),
        P("ctx", "exp"),
        P("exp", "ctx"),
        P(("ctx", "exp"), None),
        P(),
        P(("ctx", "exp"), None),
        P(("ctx", "exp"), None),
        P(("ctx", "exp"), None),
        P("exp", None),
        P("exp", None, "ctx"),
        P("exp", None, "ctx"),
        P("exp", "ctx", None),
    )
    return jax.shard_map(
        body,
        mesh=mesh,
        in_specs=placed,
        out_specs=(P("ctx", "exp"), P("ctx", "exp"), P("ctx", "exp")),
        check_vma=False,
    )
```

profile of v0, /device:TPU:2, one launch (start us, length us, event | category | flops | bytes accessed | tf_op | source)
XLA Modules:
  0.0 386.1 jit_solution(18143667295432726540)
XLA Ops:
  18.4 2.3 mul.203
  23.2 2.2 convolution_convert_fusion
  25.4 2.9 reshape.141
  28.3 20.9 %all_to_all.10 = bf16[32,2,6144]{2,1,0:T(2,128)(2,1)} all-to-all(bf16[32,2,6144]{2,1,0:T(2,128)(2,1)} %reshape.141), channel_id=1, replica_groups=mesh['ctx'=8,'exp'=32] {'exp'}, dimensions={0} | all-to-all | bytes 1572864 | tf_op jit(solution)/shard_map/all_to_all | solution.py:162
  49.2 3.0 reshape.142
  52.4 74.6 %all-gather.5.cloned.1.call-done = bf16[512,6144]{1,0:T(8,128)(2,1)} async-done(((bf16[64,6144]{1,0:T(8,128)(2,1)}), bf16[512,6144]{1,0:T(8,128)(2,1)}) %all-gather.5.cloned.1.call-update) | async-done | bytes 6291472 | tf_op jit(solution)/shard_map/all_gather | solution.py:166
  127.0 6.1 %fusion.2 = f32[512,576]{0,1:T(8,128)} fusion(bf16[1,3072,576]{1,2,0:T(8,128)(2,1)} %param.27, bf16[512,6144]{1,0:T(8,128)(2,1)} %all-gather.5.cloned.1.call-done), kind=kOutput, calls=%fused_computation.6 | convolution fusion | flops 1811939328 | bytes 7864320 | tf_op jit(solution)/shard_map/dot_general | solution.py:43
  133.1 3.1 fusion.7
  136.2 11.1 %fusion = f32[512,3072]{1,0:T(8,128)} fusion(bf16[1,3072,576]{1,2,0:T(8,128)(2,1)} %param.27, f32[512,576]{0,1:T(8,128)} %fusion.7, bf16[1,3072,576]{1,2,0:T(8,128)(2,1)S(1)} %copy-done, bf16[512,6144]{1,0:T(8,128)(2,1)} %all-gather.5.cloned.1.call-done, f32[512,576]{0,1:T(8,128)} %fusion.2), kind=kOutput, calls=%fused_computation.4 | convolution fusion | flops 3626827776 | bytes 18874368 | tf_op jit(solution)/shard_map/dot_general | solution.py:53
  147.3 6.8 %add_convert_fusion = bf16[512,3072]{1,0:T(8,128)(2,1)} fusion(f32[512,3072]{1,0:T(8,128)} %fusion, bf16[1,3072,576]{1,2,0:T(8,128)(2,1)S(1)} %copy-done, f32[512,576]{0,1:T(8,128)} %fusion.7, f32[512,576]{0,1:T(8,128)} %fusion.2), kind=kOutput, calls=%fused_computation.3 | convolution fusion | flops 1816854528 | bytes 15335424 | tf_op jit(solution)/shard_map/dot_general | solution.py:56
  154.1 7.2 %convert_element_type.79 = bf16[8,32,2,3072]{3,2,1,0:T(2,128)(2,1)} reshape(bf16[512,3072]{1,0:T(8,128)(2,1)} %add_convert_fusion) | data formatting | bytes 6291456 | tf_op jit(solution)/shard_map/convert_element_type | solution.py:170
  161.3 4.4 %copy.34 = bf16[8,32,2,3072]{3,1,2,0:T(8,128)(2,1)} copy(bf16[8,32,2,3072]{3,2,1,0:T(2,128)(2,1)} %convert_element_type.79) | data formatting | bytes 6291456 | tf_op jit(solution)/shard_map/convert_element_type | solution.py:170
  165.7 45.8 %reduce-scatter.2.cloned.1.call-done = bf16[1,32,2,3072]{3,1,2,0:T(8,128)(2,1)} async-done(((bf16[8,32,2,3072]{3,1,2,0:T(8,128)(2,1)}), bf16[1,32,2,3072]{3,1,2,0:T(8,128)(2,1)}) %reduce-scatter.2.cloned.1.call-update) | async-done | bytes 393232 | tf_op jit(solution)/shard_map/reduce_scatter | solution.py:169
  211.6 2.1 copy.35
  213.7 7.3 %all-to-all-start.1 = ((bf16[32,2,3072]{2,1,0:T(2,128)(2,1)}), bf16[32,2,3072]{2,1,0:T(2,128)(2,1)}, u32[]{:S(2)}, u32[]{:S(2)}) async-start(bf16[32,2,3072]{2,1,0:T(2,128)(2,1)} %copy.35), calls=%async_computation.2 | async-start | bytes 786432 | tf_op jit(solution)/shard_map/all_to_all | solution.py:172
  223.7 6.3 %all-to-all-done.1 = bf16[32,2,3072]{2,1,0:T(2,128)(2,1)} async-done(((bf16[32,2,3072]{2,1,0:T(2,128)(2,1)}), bf16[32,2,3072]{2,1,0:T(2,128)(2,1)}, u32[]{:S(2)}, u32[]{:S(2)}) %all-to-all-start.1) | async-done | bytes 393248 | tf_op jit(solution)/shard_map/all_to_all | solution.py:172
  230.0 1.9 reshape.153
  240.6 16.3 %all-reduce = f32[8]{0:T(128)} all-reduce(f32[8]{0:T(128)S(1)} %dynamic-update-slice), channel_id=1, replica_groups=mesh['ctx'=8,'exp'=32] {'ctx'}, use_global_device_ids=true, to_apply=%add | all-reduce | flops 8 | bytes 64
  259.1 27.3 %all-gather = f32[1024,128]{1,0:T(8,128)} all-gather(f32[128,128]{1,0:T(8,128)S(1)} %fusion.53), channel_id=2, replica_groups=mesh['ctx'=8,'exp'=32] {'ctx'}, dimensions={0}, use_global_device_ids=true | all-gather | bytes 589824 | tf_op jit(solution)/shard_map/all_gather | solution.py:12
  287.0 4.0 %convolution_convert_fusion.1 = bf16[768,128]{1,0:T(8,128)(2,1)S(1)} fusion(bf16[768,3072]{1,0:T(8,128)(2,1)} %all-gather.7.cloned.1.call-done, bf16[128,3072]{1,0:T(8,128)(2,1)} %param.26), kind=kOutput, calls=%fused_computation.42 | convolution fusion | flops 604078080 | bytes 5701632 | tf_op jit(solution)/shard_map/dot_general | solution.py:188
  293.2 3.2 fusion.22
  298.1 49.7 %all-gather.1 = f32[1024,128]{1,0:T(8,128)} all-gather(f32[128,128]{1,0:T(8,128)S(1)} %convolution_multiply_fusion.3), channel_id=3, replica_groups=mesh['ctx'=8,'exp'=32] {'ctx'}, dimensions={0}, use_global_device_ids=true | all-gather | bytes 589824 | tf_op jit(solution)/shard_map/all_gather | solution.py:12
  348.4 23.6 %while.27 = (s32[]{:T(128)}, f32[128,128]{1,0:T(8,128)}, s32[]{:T(128)}, f32[8]{0:T(128)}, f32[8,128,128]{2,1,0:T(8,128)}, /*index=5*/s32[]{:T(128)}, s32[]{:T(128)}, s32[]{:T(128)}, s32[]{:T(128)}) while((s32[]{:T(128)}, f32[128,128]{1,0:T(8,128)}, s32[]{:T(128)}, f32[8]{0:T(128)}, f32[8,128,128]{2,1,0:T(8,128)}, /*index=5*/s32[]{:T(128)}, ...), condition=%wide.region_11.12_spmd, body=%wide.region_10.11_spmd.sunk | while | flops 32774 | bytes 196767 | solution.py:21
  349.6 2.2 bitcast_add_fusion.5
  353.0 2.2 bitcast_add_fusion.5
  356.4 2.2 bitcast_add_fusion.5
  359.8 2.2 bitcast_add_fusion.5
  363.1 2.2 bitcast_add_fusion.5
  366.5 2.2 bitcast_add_fusion.5
  369.9 2.2 bitcast_add_fusion.5
  373.5 2.1 fusion.42
  375.6 2.5 fusion.41
  (75 shorter events, 43.4 us)
Async XLA Ops:
  7.2 129.1 %copy-start = (bf16[1,3072,576]{1,2,0:T(8,128)(2,1)S(1)}, bf16[1,3072,576]{1,2,0:T(8,128)(2,1)}, u32[]{:S(2)}) copy-start(bf16[1,3072,576]{1,2,0:T(8,128)(2,1)} %param.28) | copy-start | bytes 10616836
  7.2 119.8 %all-gather.5.cloned.1.call-start = ((), (), s32[]{:S(2)}) async-start(), calls=%async_computation.3 | async-start | bytes 7077888 | tf_op jit(solution)/shard_map/all_gather | solution.py:166
  52.2 159.4 %reduce-scatter.2.cloned.1.call-start = ((), (), s32[]{:S(2)}) async-start(), calls=%async_computation.4 | async-start | bytes 3538944 | tf_op jit(solution)/shard_map/reduce_scatter | solution.py:169
  127.0 6.1 %copy-start.8 = (bf16[512,6144]{1,0:T(8,128)(2,1)S(1)}, bf16[512,6144]{1,0:T(8,128)(2,1)}, u32[]{:S(2)}) copy-start(bf16[512,6144]{1,0:T(8,128)(2,1)} %all-gather.5.cloned.1.call-done) | copy-start | bytes 18874372
  127.0 6.1 %copy-start.9 = (bf16[1,576,3072]{2,1,0:T(8,128)(2,1)S(1)}, bf16[1,576,3072]{2,1,0:T(8,128)(2,1)}, u32[]{:S(2)}) copy-start(bf16[1,576,3072]{2,1,0:T(8,128)(2,1)} %param.29) | copy-start | bytes 10616836
  165.7 67.5 %copy-start.7 = (f32[3072]{0:T(1024)S(1)}, f32[3072]{0:T(1024)}, u32[]{:S(2)}) copy-start(f32[3072]{0:T(1024)} %param.22) | copy-start | bytes 36868
  213.7 16.3 %all-to-all-start.1 = ((bf16[32,2,3072]{2,1,0:T(2,128)(2,1)}), bf16[32,2,3072]{2,1,0:T(2,128)(2,1)}, u32[]{:S(2)}, u32[]{:S(2)}) async-start(bf16[32,2,3072]{2,1,0:T(2,128)(2,1)} %copy.35), calls=%async_computation.2 | async-start | bytes 786432 | tf_op jit(solution)/shard_map/all_to_all | solution.py:172
  221.0 66.0 %all-gather.7.cloned.1.call-start = ((), (), s32[]{:S(2)}) async-start(), calls=%async_computation.5 | async-start | bytes 4866048 | tf_op jit(solution)/shard_map/all_gather | solution.py:189
  287.0 4.7 %copy-start.4 = (bf16[768,128]{1,0:T(8,128)(2,1)S(1)}, bf16[768,128]{1,0:T(8,128)(2,1)}, u32[]{:S(2)}) copy-start(bf16[768,128]{1,0:T(8,128)(2,1)} %param.19) | copy-start | bytes 589828
  291.0 0.7 copy-start.5
  372.0 6.0 %copy-start.2 = (f32[128,128]{1,0:T(8,128)S(1)}, f32[128,128]{1,0:T(8,128)}, u32[]{:S(2)}) copy-start(f32[128,128]{1,0:T(8,128)} %get-tuple-element.131) | copy-start | bytes 196612
  372.0 6.0 %copy-start.6 = (bf16[768,128]{1,0:T(8,128)(2,1)S(1)}, bf16[768,128]{1,0:T(8,128)(2,1)}, u32[]{:S(2)}) copy-start(bf16[768,128]{1,0:T(8,128)(2,1)} %copy-done.5) | copy-start | bytes 589828
  372.0 6.4 %copy-start.1 = (bf16[768,768]{1,0:T(8,128)(2,1)S(1)}, bf16[768,768]{1,0:T(8,128)(2,1)}, u32[]{:S(2)}) copy-start(bf16[768,768]{1,0:T(8,128)(2,1)} %multiply_convert_fusion.1) | copy-start | bytes 3538948
  372.0 6.4 %copy-start.3 = (bf16[768,128]{1,0:T(8,128)(2,1)S(1)}, bf16[768,128]{1,0:T(8,128)(2,1)}, u32[]{:S(2)}) copy-start(bf16[768,128]{1,0:T(8,128)(2,1)} %param.18) | copy-start | bytes 589828
Sparse Core Ops, SparseCore 0:
  52.3 74.6 all-gather.4
  165.9 45.6 reduce-scatter.1
  236.2 48.4 all-gather.6
where the time goes:
time: 388 us; the launch traced here: 386 us
  waiting for transfers between devices  127 us (33%)
  blocking collectives  114 us (29%)
  matrix products  50 us (13%)
  local copies, waits for them, and re-layouts  45.2 us (12%)
  other arithmetic  27.8 us (7%)
  between operations  14.5 us (4%)
  starting transfers between devices  7.6 us (2%)
    all_gather x2, blocking collectives, prefix(): gathered = jax.tree.map(lambda a: lax.all_gather(a, axis), part)  77 us
    all_gather x1, waiting for transfers between devices, body(): lax.all_gather(arrived, 'ctx', axis=0, tiled=True)  74.6 us
    reduce_scatter x1, waiting for transfers between devices, body(): lax.psum_scatter(partials.astype(jnp.bfloat16), 'ctx', scatter_dimension=...  45.8 us
    all_to_all x1, blocking collectives, body(): lax.all_to_all(outgoing, 'exp', split_axis=0, concat_axis=0, tiled=True)  20.9 us
    unnamed x1, blocking collectives  16.3 us
    add x7, other arithmetic, chain_link(): return (earlier[0] * following[0], following[0] * earlier[1] + following[1])  15.1 us
    convert_element_type x2, local copies, waits for them, and re-layouts, body(): partials.astype(jnp.bfloat16)  11.6 us
    dot_general x1, matrix products, expert_rows(): lax.dot_general(gate_grad, gate_mat, (((1,), (1,)), ((), ())), preferred_...  11.1 us
  transfers between devices with their start and end apart: 4, of which 3 were waited for; matrix products, arithmetic and copies ran while one was open for 2% of the time, Pallas kernels for 0%

commit v1 on v0

--- a/solution.py
+++ b/solution.py
@@ -3,6 +3,14 @@
 import jax.numpy as jnp
 from jax import lax
 from jax.sharding import PartitionSpec as P
+
+
+def gather_from_all(value, axis, dim):
+    count = lax.axis_size(axis)
+    repeats = [count if d == dim else 1 for d in range(value.ndim)]
+    return lax.all_to_all(
+        jnp.tile(value, repeats), axis, split_axis=dim, concat_axis=dim, tiled=True
+    )
 
 
 def prefix(part, axis, combine, identity, reverse):
@@ -162,9 +170,7 @@
     arrived = lax.all_to_all(outgoing, "exp", split_axis=0, concat_axis=0, tiled=True).reshape(
         exp_count * capacity, 2 * features
     )
-    partials = expert_rows(
-        lax.all_gather(arrived, "ctx", axis=0, tiled=True), gate_mat, up_mat, down_mat
-    )
+    partials = expert_rows(gather_from_all(arrived, "ctx", 0), gate_mat, up_mat, down_mat)
     partials = partials.reshape(ctx_count, exp_count, capacity, features)
     summed = lax.psum_scatter(
         partials.astype(jnp.bfloat16), "ctx", scatter_dimension=0, tiled=True

time: 388 us -> 459 us (1.18)
  blocking collectives: 114 us -> 264 us
  waiting for transfers between devices: 127 us -> 47.2 us
    all_to_all x0 -> x1, blocking collectives: none -> 150 us  [gather_from_all(): lax.all_to_all(jnp.tile(value, repeats), axis, split_axis=dim, concat_axi...]
    all_gather x1 -> x0, waiting for transfers between devices: 74.6 us -> none  [body(): lax.all_gather(arrived, 'ctx', axis=0, tiled=True)]
    reduce_scatter x1, waiting for transfers between devices: 45.8 us -> 40.9 us  [body(): lax.psum_scatter(partials.astype(jnp.bfloat16), 'ctx', scatter_dimension=...]
    another operation x1 -> x3, local copies, waits for them, and re-layouts: 0.12 us -> 4.97 us  [the longest x2 4.85 us: gather_from_all(): jnp.tile(value, repeats)]
  transfers between devices with their start and end apart: 4 -> 3, of which waited for: 3 -> 2; matrix products, arithmetic and copies ran while one was open for 2% -> 2% of each run, Pallas kernels for 0% -> 0%
where the time goes in v1:
time: 459 us; the launch traced here: 457 us
  blocking collectives  264 us (58%)
  local copies, waits for them, and re-layouts  48.7 us (11%)
  waiting for transfers between devices  47.2 us (10%)
  matrix products  47 us (10%)
  other arithmetic  27.7 us (6%)
  between operations  14.8 us (3%)
  starting transfers between devices  7.51 us (2%)
    all_to_all x1, blocking collectives, gather_from_all(): lax.all_to_all(jnp.tile(value, repeats), axis, split_axis=dim, concat_axi...  150 us
    all_gather x2, blocking collectives, prefix(): gathered = jax.tree.map(lambda a: lax.all_gather(a, axis), part)  77.1 us
    reduce_scatter x1, waiting for transfers between devices, body(): lax.psum_scatter(partials.astype(jnp.bfloat16), 'ctx', scatter_dimension=...  40.9 us
    all_to_all x1, blocking collectives, body(): lax.all_to_all(outgoing, 'exp', split_axis=0, concat_axis=0, tiled=True)  20.9 us
    unnamed x1, blocking collectives  16.1 us
    add x7, other arithmetic, chain_link(): return (earlier[0] * following[0], following[0] * earlier[1] + following[1])  15.1 us
    convert_element_type x2, local copies, waits for them, and re-layouts, body(): partials.astype(jnp.bfloat16)  11.7 us
    dot_general x1, matrix products, expert_rows(): lax.dot_general(gate_grad, gate_mat, (((1,), (1,)), ((), ())), preferred_...  11.1 us
  transfers between devices with their start and end apart: 3, of which 2 were waited for; matrix products, arithmetic and copies ran while one was open for 2% of the time, Pallas kernels for 0%

profile of v1, /device:TPU:2, one launch (start us, length us, event | category | flops | bytes accessed | tf_op | source)
XLA Modules:
  0.0 457.3 jit_solution(12713695408041742184)
XLA Ops:
  18.4 2.3 mul.203
  23.2 2.2 convolution_convert_fusion
  25.4 2.9 reshape.145
  28.3 20.9 %all_to_all.19 = bf16[32,2,6144]{2,1,0:T(2,128)(2,1)} all-to-all(bf16[32,2,6144]{2,1,0:T(2,128)(2,1)} %reshape.145), channel_id=1, replica_groups=mesh['ctx'=8,'exp'=32] {'exp'}, dimensions={0} | all-to-all | bytes 1572864 | tf_op jit(solution)/shard_map/all_to_all | solution.py:170
  49.2 3.0 tile.8
  54.0 150.1 %all_to_all.20 = bf16[8,64,6144]{2,1,0:T(8,128)(2,1)S(1)} all-to-all(bf16[8,64,6144]{2,1,0:T(8,128)(2,1)S(1)} %tile.9), channel_id=1, replica_groups=mesh['ctx'=8,'exp'=32] {'ctx'}, dimensions={0} | all-to-all | bytes 12582912 | tf_op jit(solution)/shard_map/all_to_all | solution.py:11
  204.2 3.0 fusion.2
  208.8 3.1 fusion.7
  211.9 11.1 %fusion = f32[512,3072]{1,0:T(8,128)} fusion(bf16[1,3072,576]{1,2,0:T(8,128)(2,1)} %param.27, f32[512,576]{0,1:T(8,128)} %fusion.7, bf16[1,3072,576]{1,2,0:T(8,128)(2,1)S(1)} %copy-done, bf16[512,6144]{1,0:T(8,128)(2,1)} %bitcast.78, f32[512,576]{0,1:T(8,128)} %fusion.2), kind=kOutput, calls=%fused_computation.4 | convolution fusion | flops 3626827776 | bytes 18874368 | tf_op jit(solution)/shard_map/dot_general | solution.py:61
  223.0 6.9 %add_convert_fusion = bf16[512,3072]{1,0:T(8,128)(2,1)} fusion(f32[512,3072]{1,0:T(8,128)} %fusion, bf16[1,3072,576]{1,2,0:T(8,128)(2,1)S(1)} %copy-done, f32[512,576]{0,1:T(8,128)} %fusion.7, f32[512,576]{0,1:T(8,128)} %fusion.2), kind=kOutput, calls=%fused_computation.3 | convolution fusion | flops 1816854528 | bytes 15335424 | tf_op jit(solution)/shard_map/dot_general | solution.py:64
  229.8 7.2 %convert_element_type.79 = bf16[8,32,2,3072]{3,2,1,0:T(2,128)(2,1)} reshape(bf16[512,3072]{1,0:T(8,128)(2,1)} %add_convert_fusion) | data formatting | bytes 6291456 | tf_op jit(solution)/shard_map/convert_element_type | solution.py:176
  237.1 4.4 copy.34
  241.5 40.9 %reduce-scatter.2.cloned.1.call-done = bf16[1,32,2,3072]{3,1,2,0:T(8,128)(2,1)} async-done(((bf16[8,32,2,3072]{3,1,2,0:T(8,128)(2,1)}), bf16[1,32,2,3072]{3,1,2,0:T(8,128)(2,1)}) %reduce-scatter.2.cloned.1.call-update) | async-done | bytes 393232 | tf_op jit(solution)/shard_map/reduce_scatter | solution.py:175
  282.4 2.1 copy.35
  284.5 7.4 %all-to-all-start.2 = ((bf16[32,2,3072]{2,1,0:T(2,128)(2,1)}), bf16[32,2,3072]{2,1,0:T(2,128)(2,1)}, u32[]{:S(2)}, u32[]{:S(2)}) async-start(bf16[32,2,3072]{2,1,0:T(2,128)(2,1)} %copy.35), calls=%async_computation.3 | async-start | bytes 786432 | tf_op jit(solution)/shard_map/all_to_all | solution.py:178
  294.6 6.3 %all-to-all-done.2 = bf16[32,2,3072]{2,1,0:T(2,128)(2,1)} async-done(((bf16[32,2,3072]{2,1,0:T(2,128)(2,1)}), bf16[32,2,3072]{2,1,0:T(2,128)(2,1)}, u32[]{:S(2)}, u32[]{:S(2)}) %all-to-all-start.2) | async-done | bytes 393248 | tf_op jit(solution)/shard_map/all_to_all | solution.py:178
  301.0 1.9 reshape.156
  311.6 16.1 %all-reduce = f32[8]{0:T(128)} all-reduce(f32[8]{0:T(128)S(1)} %dynamic-update-slice), channel_id=1, replica_groups=mesh['ctx'=8,'exp'=32] {'ctx'}, use_global_device_ids=true, to_apply=%add | all-reduce | flops 8 | bytes 64
  329.9 27.3 %all-gather = f32[1024,128]{1,0:T(8,128)} all-gather(f32[128,128]{1,0:T(8,128)S(1)} %fusion.53), channel_id=2, replica_groups=mesh['ctx'=8,'exp'=32] {'ctx'}, dimensions={0}, use_global_device_ids=true | all-gather | bytes 589824 | tf_op jit(solution)/shard_map/all_gather | solution.py:20
  357.8 4.0 convolution_convert_fusion.1
  364.0 3.2 fusion.22
  368.9 49.8 %all-gather.1 = f32[1024,128]{1,0:T(8,128)} all-gather(f32[128,128]{1,0:T(8,128)S(1)} %convolution_multiply_fusion.3), channel_id=3, replica_groups=mesh['ctx'=8,'exp'=32] {'ctx'}, dimensions={0}, use_global_device_ids=true | all-gather | bytes 589824 | tf_op jit(solution)/shard_map/all_gather | solution.py:20
  419.3 23.6 %while.27 = (s32[]{:T(128)}, f32[128,128]{1,0:T(8,128)}, s32[]{:T(128)}, f32[8]{0:T(128)}, f32[8,128,128]{2,1,0:T(8,128)}, /*index=5*/s32[]{:T(128)}, s32[]{:T(128)}, s32[]{:T(128)}, s32[]{:T(128)}) while((s32[]{:T(128)}, f32[128,128]{1,0:T(8,128)}, s32[]{:T(128)}, f32[8]{0:T(128)}, f32[8,128,128]{2,1,0:T(8,128)}, /*index=5*/s32[]{:T(128)}, ...), condition=%wide.region_11.12_spmd, body=%wide.region_10.11_spmd.sunk | while | flops 32774 | bytes 196767 | solution.py:29
  420.5 2.2 bitcast_add_fusion.5
  423.9 2.2 bitcast_add_fusion.5
  427.2 2.2 bitcast_add_fusion.5
  430.6 2.2 bitcast_add_fusion.5
  434.0 2.2 bitcast_add_fusion.5
  437.3 2.2 bitcast_add_fusion.5
  440.7 2.2 bitcast_add_fusion.5
  444.3 2.1 fusion.42
  446.4 2.5 fusion.41
  (76 shorter events, 46.6 us)
Async XLA Ops:
  7.2 204.7 %copy-start = (bf16[1,3072,576]{1,2,0:T(8,128)(2,1)S(1)}, bf16[1,3072,576]{1,2,0:T(8,128)(2,1)}, u32[]{:S(2)}) copy-start(bf16[1,3072,576]{1,2,0:T(8,128)(2,1)} %param.28) | copy-start | bytes 10616836
  7.2 275.2 %reduce-scatter.2.cloned.1.call-start = ((), (), s32[]{:S(2)}) async-start(), calls=%async_computation.4 | async-start | bytes 3538944 | tf_op jit(solution)/shard_map/reduce_scatter | solution.py:175
  54.0 150.2 %copy-start.10 = (bf16[1,3072,576]{1,2,0:T(8,128)(2,1)S(1)}, bf16[1,3072,576]{1,2,0:T(8,128)(2,1)}, u32[]{:S(2)}) copy-start(bf16[1,3072,576]{1,2,0:T(8,128)(2,1)} %param.27) | copy-start | bytes 10616836
  204.2 3.7 copy-start.1
  204.2 4.6 %copy-start.9 = (bf16[1,576,3072]{2,1,0:T(8,128)(2,1)S(1)}, bf16[1,576,3072]{2,1,0:T(8,128)(2,1)}, u32[]{:S(2)}) copy-start(bf16[1,576,3072]{2,1,0:T(8,128)(2,1)} %param.29) | copy-start | bytes 10616836
  241.5 62.7 %copy-start.8 = (f32[3072]{0:T(1024)S(1)}, f32[3072]{0:T(1024)}, u32[]{:S(2)}) copy-start(f32[3072]{0:T(1024)} %param.22) | copy-start | bytes 36868
  284.5 16.5 %all-to-all-start.2 = ((bf16[32,2,3072]{2,1,0:T(2,128)(2,1)}), bf16[32,2,3072]{2,1,0:T(2,128)(2,1)}, u32[]{:S(2)}, u32[]{:S(2)}) async-start(bf16[32,2,3072]{2,1,0:T(2,128)(2,1)} %copy.35), calls=%async_computation.3 | async-start | bytes 786432 | tf_op jit(solution)/shard_map/all_to_all | solution.py:178
  292.0 65.9 %all-gather.4.cloned.1.call-start = ((), (), s32[]{:S(2)}) async-start(), calls=%async_computation.5 | async-start | bytes 4866048 | tf_op jit(solution)/shard_map/all_gather | solution.py:195
  357.8 4.7 %copy-start.5 = (bf16[768,128]{1,0:T(8,128)(2,1)S(1)}, bf16[768,128]{1,0:T(8,128)(2,1)}, u32[]{:S(2)}) copy-start(bf16[768,128]{1,0:T(8,128)(2,1)} %param.19) | copy-start | bytes 589828
  361.8 0.7 copy-start.6
  442.9 6.0 %copy-start.3 = (f32[128,128]{1,0:T(8,128)S(1)}, f32[128,128]{1,0:T(8,128)}, u32[]{:S(2)}) copy-start(f32[128,128]{1,0:T(8,128)} %get-tuple-element.131) | copy-start | bytes 196612
  442.9 6.0 %copy-start.7 = (bf16[768,128]{1,0:T(8,128)(2,1)S(1)}, bf16[768,128]{1,0:T(8,128)(2,1)}, u32[]{:S(2)}) copy-start(bf16[768,128]{1,0:T(8,128)(2,1)} %copy-done.6) | copy-start | bytes 589828
  442.9 6.4 %copy-start.2 = (bf16[768,768]{1,0:T(8,128)(2,1)S(1)}, bf16[768,768]{1,0:T(8,128)(2,1)}, u32[]{:S(2)}) copy-start(bf16[768,768]{1,0:T(8,128)(2,1)} %multiply_convert_fusion.1) | copy-start | bytes 3538948
  442.9 6.4 %copy-start.4 = (bf16[768,128]{1,0:T(8,128)(2,1)S(1)}, bf16[768,128]{1,0:T(8,128)(2,1)}, u32[]{:S(2)}) copy-start(bf16[768,128]{1,0:T(8,128)(2,1)} %param.18) | copy-start | bytes 589828
Sparse Core Ops, SparseCore 0:
  241.6 40.6 reduce-scatter.1
  307.2 48.2 all-gather.3
